TPU v7x, 32 devices: a whole 2x2x4 slice. The times are simulated.
32 devices in a mesh: ctx: 8 (over z, x), head: 4 (over y, core).
Axes of the slice: x: 2, y: 2, z: 4, core: 2. Of those that a mesh axis runs over, the one named last changes fastest.
Arguments:
- query_rows: bfloat16 [8192, 6144], P(('ctx', 'head')), may hold values from -0.52734375 to 0.52734375
- key_rows: bfloat16 [8192, 6144], P(('ctx', 'head')), may hold values from -0.52734375 to 0.52734375
- value_rows: bfloat16 [8192, 6144], P(('ctx', 'head')), may hold values from -0.62890625 to 0.62890625
- grad_out: bfloat16 [8192, 6144], P(('ctx', 'head')), may hold values from -0.62890625 to 0.62890625
- decay_rates: float32 [48], replicated, as said below
Outputs:
- query_gradient: bfloat16 [8192, 6144], P(('ctx', 'head'))
- grad_key: bfloat16 [8192, 6144], P(('ctx', 'head'))
- value_gradient: bfloat16 [8192, 6144], P(('ctx', 'head'))
Inputs may be any that keep to these rules, and one draw needn't show every extreme that they name: decay_rates lie between 0.1 / 8192 and 24 / 256.
All inputs are finite; a program needn't handle non-finite values.
Results may differ from a plain program's by a relative error of at most 0.0056.
Values may be sent and summed in bfloat16 or wider, within the bound.
No kernel may reach another device: no remote copies, remote signals or barrier semaphores. Data moves between devices by JAX's collectives and lax.ppermute only.
A program may use at most 128 MiB of HBM per device.

v0:
```python
import jax
import jax.numpy as jnp
from jax import lax
from jax.sharding import PartitionSpec as P

DH = 128
BLOCK = 256
HIGHEST = lax.Precision.HIGHEST


def carried_in(value, axis, join, neutral, backward):
    count, mine = (lax.axis_size(axis), lax.axis_index(axis))
    pieces = jax.tree.map(lambda part: lax.all_gather(part, axis), value)
    if backward:
        pieces = jax.tree.map(lambda part: part[::-1], pieces)
        mine = count - 1 - mine
    subtotal = jax.tree.map(
        lambda part, zero: jnp.full_like(part, 0) + jnp.asarray(zero, part.dtype), value, neutral
    )

    def lap(position, subtotal):
        longer = join(subtotal, jax.tree.map(lambda part: part[position], pieces))
        return jax.tree.map(lambda new, old: jnp.where(position < mine, new, old), longer, subtotal)

    return lax.fori_loop(0, count - 1, lap, subtotal)


def combine_states(earlier, later):
    decay_early, state_early = earlier
    decay_late, state_late = later
    return (decay_early * decay_late, decay_late[:, None, None] * state_early + state_late)


def local(query_rows, key_rows, value_rows, grad_out, decay_rates):
    queries, keys_here, values, grads = (
        lax.all_to_all(query_rows, "head", split_axis=1, concat_axis=0, tiled=True),
        lax.all_to_all(key_rows, "head", split_axis=1, concat_axis=0, tiled=True),
        lax.all_to_all(value_rows, "head", split_axis=1, concat_axis=0, tiled=True),
        lax.all_to_all(grad_out, "head", split_axis=1, concat_axis=0, tiled=True),
    )
    rows = queries.shape[0]
    heads_here = queries.shape[1] // DH
    nblocks = rows // BLOCK
    rates = lax.dynamic_slice_in_dim(
        decay_rates, lax.axis_index("head") * heads_here, heads_here, 0
    )
    shape_four = (nblocks, BLOCK, heads_here, DH)
    q_blocks = queries.reshape(shape_four)
    key_block_list = keys_here.reshape(shape_four)
    v_blocks = values.reshape(shape_four)
    gradient_block_list = grads.reshape(shape_four)
    position = jnp.arange(BLOCK, dtype=jnp.float32)
    offset = position[:, None] - position[None, :]
    decay_mask = jnp.where(
        offset[None] >= 0.0, jnp.exp(-rates[:, None, None] * jnp.maximum(offset, 0.0)[None]), 0.0
    )
    grad_scores = jnp.einsum(
        "nihd,njhd->nhij", gradient_block_list, v_blocks, preferred_element_type=jnp.float32
    )
    weight_gradient_set = (grad_scores * decay_mask[None]).astype(jnp.bfloat16)
    fwd_scores = jnp.einsum(
        "nihd,njhd->nhij", q_blocks, key_block_list, preferred_element_type=jnp.float32
    )
    forward_weight_set = (fwd_scores * decay_mask[None]).astype(jnp.bfloat16)
    key_decay = jnp.exp(-rates[None, :] * (BLOCK - 1.0 - position)[:, None])
    query_decay = jnp.exp(-rates[None, :] * position[:, None])
    keys_decayed = (key_block_list * key_decay[None, :, :, None]).astype(jnp.bfloat16)
    decayed_query_rows = (q_blocks * query_decay[None, :, :, None]).astype(jnp.bfloat16)
    block_kv = jnp.einsum(
        "njhd,njhe->nhde", keys_decayed, v_blocks, preferred_element_type=jnp.float32
    )
    query_decay_block = jnp.einsum(
        "nihd,nihe->nhde",
        decayed_query_rows,
        gradient_block_list,
        preferred_element_type=jnp.float32,
    )
    block_index = jnp.arange(nblocks, dtype=jnp.float32)
    block_gap = block_index[:, None] - block_index[None, :]
    fwd_inside = jnp.where(
        block_gap[None] >= 1.0,
        jnp.exp(-rates[:, None, None] * BLOCK * jnp.maximum(block_gap - 1.0, 0.0)[None]),
        0.0,
    )
    rev_inside = jnp.where(
        block_gap[None] <= -1.0,
        jnp.exp(-rates[:, None, None] * BLOCK * jnp.maximum(-block_gap - 1.0, 0.0)[None]),
        0.0,
    )
    start_power = jnp.exp(-rates[:, None] * BLOCK * block_index[None, :])
    end_power = jnp.exp(-rates[:, None] * BLOCK * (nblocks - 1.0 - block_index)[None, :])
    local_fwd = jnp.einsum("hm,mhde->hde", end_power, block_kv, precision=HIGHEST)
    local_rev = jnp.einsum("hm,mhde->hde", start_power, query_decay_block, precision=HIGHEST)
    device_span = jnp.exp(-rates * rows)
    identity = (jnp.ones((heads_here,), jnp.float32), jnp.zeros((heads_here, DH, DH), jnp.float32))
    before_device = carried_in((device_span, local_fwd), "ctx", combine_states, identity, False)[1]
    after_device = carried_in((device_span, local_rev), "ctx", combine_states, identity, True)[1]
    state_before = jnp.einsum(
        "hnm,mhde->nhde", fwd_inside, block_kv, precision=HIGHEST
    ) + jnp.einsum("hn,hde->nhde", start_power, before_device, precision=HIGHEST)
    state_after = jnp.einsum(
        "hnm,mhde->nhde", rev_inside, query_decay_block, precision=HIGHEST
    ) + jnp.einsum("hn,hde->nhde", end_power, after_device, precision=HIGHEST)
    state_before_bfloat = state_before.astype(jnp.bfloat16)
    state_after_bfloat = state_after.astype(jnp.bfloat16)
    leading_part = jnp.exp(-rates[None, :] * (position + 1.0)[:, None])[None, :, :, None]
    trailing_part = jnp.exp(-rates[None, :] * (BLOCK - position)[:, None])[None, :, :, None]
    query_gradient = jnp.einsum(
        "nhij,njhd->nihd", weight_gradient_set, key_block_list, preferred_element_type=jnp.float32
    ) + leading_part * jnp.einsum(
        "nihe,nhde->nihd",
        gradient_block_list,
        state_before_bfloat,
        preferred_element_type=jnp.float32,
    )
    grad_key = jnp.einsum(
        "nhij,nihd->njhd", weight_gradient_set, q_blocks, preferred_element_type=jnp.float32
    ) + trailing_part * jnp.einsum(
        "njhe,nhde->njhd", v_blocks, state_after_bfloat, preferred_element_type=jnp.float32
    )
    value_gradient = jnp.einsum(
        "nhij,nihe->njhe",
        forward_weight_set,
        gradient_block_list,
        preferred_element_type=jnp.float32,
    ) + trailing_part * jnp.einsum(
        "njhd,nhde->njhe", key_block_list, state_after_bfloat, preferred_element_type=jnp.float32
    )
    flat_shape = (rows, heads_here * DH)
    return (
        lax.all_to_all(
            query_gradient.reshape(flat_shape).astype(jnp.bfloat16),
            "head",
            split_axis=0,
            concat_axis=1,
            tiled=True,
        ),
        lax.all_to_all(
            grad_key.reshape(flat_shape).astype(jnp.bfloat16),
            "head",
            split_axis=0,
            concat_axis=1,
            tiled=True,
        ),
        lax.all_to_all(
            value_gradient.reshape(flat_shape).astype(jnp.bfloat16),
            "head",
            split_axis=0,
            concat_axis=1,
            tiled=True,
        ),
    )


def solution(mesh):
    return jax.shard_map(
        local,
        mesh=mesh,
        in_specs=(
            P(("ctx", "head"), None),
            P(("ctx", "head"), None),
            P(("ctx", "head"), None),
            P(("ctx", "head"), None),
            P(),
        ),
        out_specs=(P(("ctx", "head"), None), P(("ctx", "head"), None), P(("ctx", "head"), None)),
        check_vma=False,
    )
```

profile of v0, /device:TPU:0, one launch (start us, length us, event | category | flops | bytes accessed | tf_op | source)
XLA Modules:
  0.0 421.6 jit_solution(8418679412917657691)
XLA Ops:
  20.7 32.4 %all-to-all-done = bf16[256,4,1536]{0,2,1:T(8,128)(2,1)S(1)} async-done(((bf16[256,4,1536]{0,2,1:T(8,128)(2,1)}), bf16[256,4,1536]{0,2,1:T(8,128)(2,1)S(1)}, u32[]{:S(2)}, u32[]{:S(2)}) %all-to-all-start) | async-done | bytes 3145760 | tf_op jit(solution)/shard_map/all_to_all | solution.py:39
  53.1 4.8 %all-to-all-start.4 = ((bf16[256,4,1536]{0,2,1:T(8,128)(2,1)}), bf16[256,4,1536]{0,2,1:T(8,128)(2,1)}, u32[]{:S(2)}, u32[]{:S(2)}) async-start(bf16[256,4,1536]{0,2,1:T(8,128)(2,1)} %bitcast.123), calls=%async_computation.4 | async-start | bytes 6291456 | tf_op jit(solution)/shard_map/all_to_all | solution.py:36
  59.6 35.2 %all-to-all-done.4 = bf16[256,4,1536]{0,2,1:T(8,128)(2,1)} async-done(((bf16[256,4,1536]{0,2,1:T(8,128)(2,1)}), bf16[256,4,1536]{0,2,1:T(8,128)(2,1)}, u32[]{:S(2)}, u32[]{:S(2)}) %all-to-all-start.4) | async-done | bytes 3145760 | tf_op jit(solution)/shard_map/all_to_all | solution.py:36
  99.4 7.1 %fusion.16 = f32[12,1,128,128]{3,1,2,0:T(1,128)} fusion(f32[4,12,128,128]{3,2,1,0:T(8,128)S(1)} %fusion.13, f32[12,4,1,1]{1,0,2,3:T(8,128)S(1)} %get-tuple-element.253), kind=kOutput, calls=%fused_computation.29 | convolution fusion | flops 9437184 | bytes 3932352 | tf_op jit(solution)/shard_map/hm,mhde->hde/dot_general | solution.py:93
  111.1 4.7 %all-to-all-start.1 = ((bf16[256,4,1536]{0,2,1:T(8,128)(2,1)}), bf16[256,4,1536]{0,2,1:T(8,128)(2,1)}, u32[]{:S(2)}, u32[]{:S(2)}) async-start(bf16[256,4,1536]{0,2,1:T(8,128)(2,1)} %bitcast.125), calls=%async_computation.1 | async-start | bytes 6291456 | tf_op jit(solution)/shard_map/all_to_all | solution.py:38
  120.5 32.2 %all-to-all-done.1 = bf16[256,4,1536]{0,2,1:T(8,128)(2,1)} async-done(((bf16[256,4,1536]{0,2,1:T(8,128)(2,1)}), bf16[256,4,1536]{0,2,1:T(8,128)(2,1)}, u32[]{:S(2)}, u32[]{:S(2)}) %all-to-all-start.1) | async-done | bytes 3145760 | tf_op jit(solution)/shard_map/all_to_all | solution.py:38
  152.8 40.6 %all_to_all.112 = bf16[256,4,1536]{0,2,1:T(8,128)(2,1)S(1)} all-to-all(bf16[256,4,1536]{0,2,1:T(8,128)(2,1)} %bitcast.127), channel_id=1, replica_groups=mesh['ctx'=8,'head'=4] {'head'}, dimensions={1} | all-to-all | bytes 6291456 | tf_op jit(solution)/shard_map/all_to_all | solution.py:37
  199.1 7.1 %fusion.20 = f32[12,1,128,128]{3,1,2,0:T(1,128)} fusion(f32[4,12,128,128]{3,2,1,0:T(8,128)S(1)} %fusion.12, f32[12,4,1,1]{1,0,2,3:T(8,128)S(1)} %get-tuple-element.255), kind=kOutput, calls=%fused_computation.33 | convolution fusion | flops 9437184 | bytes 3932352 | tf_op jit(solution)/shard_map/hm,mhde->hde/dot_general | solution.py:92
  206.2 23.3 %all-reduce = f32[96]{0:T(128)S(1)} all-reduce(f32[96]{0:T(128)S(1)} %get-tuple-element.249), channel_id=2, replica_groups=mesh['ctx'=8,'head'=4] {'ctx'}, use_global_device_ids=true, to_apply=%add | all-reduce | flops 96 | bytes 768
  230.3 4.9 %multiply_convert_fusion.1 = bf16[4,12,256,256]{3,2,1,0:T(8,128)(2,1)S(1)} fusion(f32[12,256,256]{2,1,0:T(8,128)S(1)} %exponential_select_fusion, bf16[4,256,12,128]{1,3,2,0:T(8,128)(2,1)S(1)} %bitcast.114, bf16[4,256,12,128]{1,3,2,0:T(8,128)(2,1)} %bitcast.5), kind=kOutput, calls=%fused_computation.7 | convolution fusion | flops 811597824 | bytes 15728640 | tf_op jit(solution)/shard_map/nihd,njhd->nhij/dot_general | solution.py:57
  237.8 5.5 %fusion.62 = f32[4,12,256,128]{2,3,1,0:T(8,128)} fusion(bf16[4,256,12,128]{1,3,2,0:T(8,128)(2,1)} %bitcast.27, bf16[4,12,256,256]{3,2,1,0:T(8,128)(2,1)S(1)} %multiply_convert_fusion.1), kind=kOutput, calls=%fused_computation.84 | convolution fusion | flops 805306368 | bytes 15728640 | tf_op jit(solution)/shard_map/nhij,nihd->njhd/dot_general | solution.py:116
  243.2 6.2 %rev.7 = f32[8,12,128,128]{3,2,1,0:T(8,128)} reverse(f32[8,12,128,128]{3,2,1,0:T(8,128)} %bitcast.129), dimensions={0} | reverse | bytes 12582912 | tf_op jit(solution)/shard_map/rev | solution.py:15
  249.5 16.9 %while.29 = (s32[]{:T(128)}, f32[12,128,128]{2,1,0:T(8,128)}, s32[]{:T(128)}, f32[8,12]{1,0:T(8,128)S(1)}, f32[8,12,128,128]{3,2,1,0:T(8,128)}, /*index=5*/s32[]{:T(128)}, s32[]{:T(128)}) while((s32[]{:T(128)}, f32[12,128,128]{2,1,0:T(8,128)}, s32[]{:T(128)}, f32[8,12]{1,0:T(8,128)S(1)}, f32[8,12,128,128]{3,2,1,0:T(8,128)}, ...), condition=%wide.region_3.4_spmd.clone, body=%wide.region_2.3_spmd.clone.sunk | while | flops 786436 | bytes 2359545 | solution.py:25
  266.4 10.8 %fusion.32 = bf16[4,12,128,128]{3,0,2,1:T(4,128)(2,1)} fusion(f32[12,4]{1,0:T(8,128)S(1)} %get-tuple-element.256, f32[12,128,128]{2,1,0:T(8,128)} %get-tuple-element.192, f32[4,12,128,128]{3,2,1,0:T(8,128)} %copy-done.4, f32[4,4]{1,0:T(4,128)S(1)} %add_maximum_fusion, f32[12]{0:T(128)S(1)} %broadcast_multiply_fusion, pred[4,4]{1,0:T(4,128)(4,1)S(1)} %fusion.57), kind=kOutput, calls=%fused_computation.39 | convolution fusion | flops 40108416 | bytes 5505344 | tf_op jit(solution)/shard_map/hnm,mhde->nhde/dot_general | solution.py:101
  281.0 6.9 %fusion.6 = bf16[4,256,12,128]{1,3,2,0:T(8,128)(2,1)} fusion(f32[4,12,256,128]{2,3,1,0:T(8,128)} %fusion.62, f32[256,12]{0,1:T(8,128)S(1)} %get-tuple-element.258, bf16[4,12,128,128]{2,3,1,0:T(8,128)(2,1)} %copy.55, bf16[4,256,12,128]{1,3,2,0:T(8,128)(2,1)} %bitcast.5), kind=kOutput, calls=%fused_computation.14 | convolution fusion | flops 407371776 | bytes 14168064 | tf_op jit(solution)/shard_map/njhe,nhde->njhd/dot_general | solution.py:118
  287.9 4.9 %all-to-all-start.5 = ((bf16[4,256,1536]{1,2,0:T(8,128)(2,1)}), bf16[4,256,1536]{1,2,0:T(8,128)(2,1)}, u32[]{:S(2)}, u32[]{:S(2)}) async-start(bf16[4,256,1536]{1,2,0:T(8,128)(2,1)} %bitcast.128), calls=%async_computation.5 | async-start | bytes 6291456 | tf_op jit(solution)/shard_map/all_to_all | solution.py:138
  292.8 8.5 %fusion.61 = f32[4,12,256,128]{2,3,1,0:T(8,128)} fusion(bf16[4,12,256,256]{3,2,1,0:T(8,128)(2,1)} %copy-done.1, bf16[4,256,12,128]{1,3,2,0:T(8,128)(2,1)} %bitcast.118), kind=kOutput, calls=%fused_computation.83 | convolution fusion | flops 805306368 | bytes 15728640 | tf_op jit(solution)/shard_map/nhij,njhd->nihd/dot_general | solution.py:108
  301.3 9.1 %fusion.2 = f32[4,12,256,128]{2,3,1,0:T(8,128)} fusion(bf16[4,256,12,128]{1,3,2,0:T(8,128)(2,1)S(1)} %bitcast.115, f32[12,256,256]{2,1,0:T(8,128)} %copy-done.2, bf16[4,256,12,128]{1,3,2,0:T(8,128)(2,1)} %bitcast.27, bf16[4,256,12,128]{1,3,2,0:T(8,128)(2,1)} %bitcast.119), kind=kOutput, calls=%fused_computation.8 | convolution fusion | flops 1616904192 | bytes 18874368 | tf_op jit(solution)/shard_map/nhij,nihe->njhe/dot_general | solution.py:121
  310.4 6.9 %fusion.4 = bf16[4,256,12,128]{1,3,2,0:T(8,128)(2,1)} fusion(f32[4,12,256,128]{2,3,1,0:T(8,128)} %fusion.2, f32[256,12]{0,1:T(8,128)S(1)} %get-tuple-element.258, bf16[4,12,128,128]{2,3,1,0:T(8,128)(2,1)} %copy.55, bf16[4,256,12,128]{1,3,2,0:T(8,128)(2,1)} %bitcast.120), kind=kOutput, calls=%fused_computation.11 | convolution fusion | flops 407371776 | bytes 14168064 | tf_op jit(solution)/shard_map/njhd,nhde->njhe/dot_general | solution.py:126
  317.3 12.2 %all-to-all-done.5 = bf16[4,256,1536]{1,2,0:T(8,128)(2,1)} async-done(((bf16[4,256,1536]{1,2,0:T(8,128)(2,1)}), bf16[4,256,1536]{1,2,0:T(8,128)(2,1)}, u32[]{:S(2)}, u32[]{:S(2)}) %all-to-all-start.5) | async-done | bytes 3145760 | tf_op jit(solution)/shard_map/all_to_all | solution.py:138
  334.2 16.9 %while.28 = (s32[]{:T(128)}, f32[12,128,128]{2,1,0:T(8,128)}, s32[]{:T(128)}, f32[8,12]{1,0:T(8,128)S(1)}, f32[8,12,128,128]{3,2,1,0:T(8,128)}, /*index=5*/s32[]{:T(128)}, s32[]{:T(128)}) while((s32[]{:T(128)}, f32[12,128,128]{2,1,0:T(8,128)}, s32[]{:T(128)}, f32[8,12]{1,0:T(8,128)S(1)}, f32[8,12,128,128]{3,2,1,0:T(8,128)}, ...), condition=%wide.region_1.2_spmd.clone, body=%wide.region_0.1_spmd.clone.sunk | while | flops 786436 | bytes 2359545 | solution.py:25
  351.2 10.0 %fusion.29 = bf16[4,12,128,128]{3,0,2,1:T(4,128)(2,1)S(1)} fusion(f32[12,4]{1,0:T(8,128)S(1)} %get-tuple-element.254, f32[12,128,128]{2,1,0:T(8,128)} %get-tuple-element.191, f32[4,12,128,128]{3,2,1,0:T(8,128)} %copy-done.3, f32[4,4]{1,0:T(4,128)S(1)} %add_maximum_fusion.1, f32[12]{0:T(128)S(1)} %broadcast_multiply_fusion, pred[4,4]{1,0:T(4,128)(4,1)S(1)} %fusion.58), kind=kOutput, calls=%fused_computation.38 | convolution fusion | flops 40108416 | bytes 5505344 | tf_op jit(solution)/shard_map/hnm,mhde->nhde/dot_general | solution.py:98
  361.1 5.6 %fusion.8 = bf16[4,256,12,128]{1,3,2,0:T(8,128)(2,1)} fusion(f32[4,12,256,128]{2,3,1,0:T(8,128)} %fusion.61, f32[256,12]{0,1:T(8,128)S(1)} %get-tuple-element.260, bf16[4,256,12,128]{1,3,2,0:T(8,128)(2,1)S(1)} %bitcast.116, bf16[4,12,128,128]{3,0,2,1:T(4,128)(2,1)S(1)} %fusion.29), kind=kOutput, calls=%fused_computation.17 | convolution fusion | flops 407371776 | bytes 14168064 | tf_op jit(solution)/shard_map/nihe,nhde->nihd/dot_general | solution.py:110
  384.2 27.6 %all-to-all-done.3 = bf16[4,256,1536]{1,2,0:T(8,128)(2,1)S(1)} async-done(((bf16[4,256,1536]{1,2,0:T(8,128)(2,1)}), bf16[4,256,1536]{1,2,0:T(8,128)(2,1)S(1)}, u32[]{:S(2)}, u32[]{:S(2)}) %all-to-all-start.3) | async-done | bytes 3145760 | tf_op jit(solution)/shard_map/all_to_all | solution.py:131
  (82 shorter events, 100.2 us)
Async XLA Ops:
  11.8 41.3 %all-to-all-start = ((bf16[256,4,1536]{0,2,1:T(8,128)(2,1)}), bf16[256,4,1536]{0,2,1:T(8,128)(2,1)S(1)}, u32[]{:S(2)}, u32[]{:S(2)}) async-start(bf16[256,4,1536]{0,2,1:T(8,128)(2,1)} %bitcast.126), calls=%async_computation | async-start | bytes 6291456 | tf_op jit(solution)/shard_map/all_to_all | solution.py:39
  53.1 4.9 %copy-start.6 = (u32[32]{0:T(128)S(1)}, u32[32]{0:T(128)}, u32[]{:S(2)}) copy-start(u32[32]{0:T(128)} %constant.87) | copy-start | bytes 388
  53.1 6.1 %copy-start.5 = (f32[48]{0:T(128)S(1)}, f32[48]{0:T(128)}, u32[]{:S(2)}) copy-start(f32[48]{0:T(128)} %param.13) | copy-start | bytes 580
  53.1 41.8 %all-to-all-start.4 = ((bf16[256,4,1536]{0,2,1:T(8,128)(2,1)}), bf16[256,4,1536]{0,2,1:T(8,128)(2,1)}, u32[]{:S(2)}, u32[]{:S(2)}) async-start(bf16[256,4,1536]{0,2,1:T(8,128)(2,1)} %bitcast.123), calls=%async_computation.4 | async-start | bytes 6291456 | tf_op jit(solution)/shard_map/all_to_all | solution.py:36
  57.9 185.4 %all-gather.8.cloned.1.call-start = ((), (), s32[]{:S(2)}) async-start(), calls=%async_computation.8 | async-start | bytes 7077888 | tf_op jit(solution)/shard_map/all_gather | solution.py:13
  97.7 1.7 copy-start.4
  111.1 41.6 %all-to-all-start.1 = ((bf16[256,4,1536]{0,2,1:T(8,128)(2,1)}), bf16[256,4,1536]{0,2,1:T(8,128)(2,1)}, u32[]{:S(2)}, u32[]{:S(2)}) async-start(bf16[256,4,1536]{0,2,1:T(8,128)(2,1)} %bitcast.125), calls=%async_computation.1 | async-start | bytes 6291456 | tf_op jit(solution)/shard_map/all_to_all | solution.py:38
  115.8 218.4 %all-gather.6.cloned.1.call-start = ((), (), s32[]{:S(2)}) async-start(), calls=%async_computation.7 | async-start | bytes 7077888 | tf_op jit(solution)/shard_map/all_gather | solution.py:13
  193.3 4.1 copy-start
  197.4 1.7 copy-start.3
  230.2 4.9 %copy-start.2 = (f32[12,256,256]{2,1,0:T(8,128)}, f32[12,256,256]{2,1,0:T(8,128)S(1)}, u32[]{:S(2)}) copy-start(f32[12,256,256]{2,1,0:T(8,128)S(1)} %exponential_select_fusion) | copy-start | bytes 9437188
  235.1 2.6 copy-start.1
  287.9 41.6 %all-to-all-start.5 = ((bf16[4,256,1536]{1,2,0:T(8,128)(2,1)}), bf16[4,256,1536]{1,2,0:T(8,128)(2,1)}, u32[]{:S(2)}, u32[]{:S(2)}) async-start(bf16[4,256,1536]{1,2,0:T(8,128)(2,1)} %bitcast.128), calls=%async_computation.5 | async-start | bytes 6291456 | tf_op jit(solution)/shard_map/all_to_all | solution.py:138
  329.6 41.6 %all-to-all-start.6 = ((bf16[4,256,1536]{1,2,0:T(8,128)(2,1)}), bf16[4,256,1536]{1,2,0:T(8,128)(2,1)}, u32[]{:S(2)}, u32[]{:S(2)}) async-start(bf16[4,256,1536]{1,2,0:T(8,128)(2,1)} %bitcast.121), calls=%async_computation.6 | async-start | bytes 6291456 | tf_op jit(solution)/shard_map/all_to_all | solution.py:145
  371.2 40.6 %all-to-all-start.3 = ((bf16[4,256,1536]{1,2,0:T(8,128)(2,1)}), bf16[4,256,1536]{1,2,0:T(8,128)(2,1)S(1)}, u32[]{:S(2)}, u32[]{:S(2)}) async-start(bf16[4,256,1536]{1,2,0:T(8,128)(2,1)} %bitcast.122), calls=%async_computation.3 | async-start | bytes 6291456 | tf_op jit(solution)/shard_map/all_to_all | solution.py:131
Sparse Core Ops, SparseCore 0:
  106.6 99.7 all-gather.7
  208.6 97.6 all-gather.5
where the time goes:
time: 424 us; the launch traced here: 422 us
  waiting for transfers between devices  144 us (34%)
  matrix products  89.2 us (21%)
  blocking collectives  63.9 us (15%)
  local copies, waits for them, and re-layouts  47.6 us (11%)
  other arithmetic  34.8 us (8%)
  starting transfers between devices  27 us (6%)
  between operations  14.9 us (4%)
    all_to_all x1, blocking collectives, local(): lax.all_to_all(key_rows, 'head', split_axis=1, concat_axis=0, tiled=True)  40.6 us
    all_to_all x1, waiting for transfers between devices, local(): lax.all_to_all(query_rows, 'head', split_axis=1, concat_axis=0, tiled=True)  35.2 us
    select_n x14, other arithmetic, lap(): jnp.where(position < mine, new, old)  33.7 us
    all_to_all x1, waiting for transfers between devices, local(): lax.all_to_all(grad_out, 'head', split_axis=1, concat_axis=0, tiled=True)  32.4 us
    all_to_all x1, waiting for transfers between devices, local(): lax.all_to_all(value_rows, 'head', split_axis=1, concat_axis=0, tiled=True)  32.2 us
    all_to_all x1, waiting for transfers between devices, local(): lax.all_to_all(query_gradient.reshape(flat_shape).astype(jnp.bfloat16), '...  27.6 us
    unnamed x1, blocking collectives  23.3 us
    unnamed x18, local copies, waits for them, and re-layouts  15.8 us
  transfers between devices with their start and end apart: 8, of which 6 were waited for; matrix products, arithmetic and copies ran while one was open for 35% of the time, Pallas kernels for 0%

commit v1 on v0

--- a/solution.py
+++ b/solution.py
@@ -128,12 +128,20 @@
     )
     flat_shape = (rows, heads_here * DH)
     return (
-        lax.all_to_all(
-            query_gradient.reshape(flat_shape).astype(jnp.bfloat16),
-            "head",
-            split_axis=0,
-            concat_axis=1,
-            tiled=True,
+        jnp.concatenate(
+            lax.all_to_all(
+                jnp.stack(
+                    jnp.split(
+                        query_gradient.reshape(flat_shape).astype(jnp.bfloat16),
+                        lax.axis_size("head"),
+                        axis=0,
+                    )
+                ),
+                "head",
+                0,
+                0,
+            ),
+            axis=1,
         ),
         lax.all_to_all(
             grad_key.reshape(flat_shape).astype(jnp.bfloat16),

time: 424 us -> 423 us (level)
  no operation moved by 1% of the time
where the time goes in v1:
time: 423 us; the launch traced here: 422 us
  waiting for transfers between devices  144 us (34%)
  matrix products  87.5 us (21%)
  blocking collectives  63.9 us (15%)
  local copies, waits for them, and re-layouts  47.8 us (11%)
  other arithmetic  36.6 us (9%)
  starting transfers between devices  27 us (6%)
  between operations  14.9 us (4%)
    all_to_all x1, blocking collectives, local(): lax.all_to_all(key_rows, 'head', split_axis=1, concat_axis=0, tiled=True)  40.6 us
    all_to_all x1, waiting for transfers between devices, local(): lax.all_to_all(query_rows, 'head', split_axis=1, concat_axis=0, tiled=True)  35.2 us
    select_n x14, other arithmetic, lap(): jnp.where(position < mine, new, old)  33.7 us
    all_to_all x1, waiting for transfers between devices, local(): lax.all_to_all(grad_out, 'head', split_axis=1, concat_axis=0, tiled=True)  32.4 us
    all_to_all x1, waiting for transfers between devices, local(): lax.all_to_all(value_rows, 'head', split_axis=1, concat_axis=0, tiled=True)  32.2 us
    all_to_all x1, waiting for transfers between devices, local(): lax.all_to_all(jnp.stack(jnp.split(query_gradient.reshape(flat_shape).ast...  27.6 us
    unnamed x1, blocking collectives  23.3 us
    unnamed x18, local copies, waits for them, and re-layouts  15.8 us
  transfers between devices with their start and end apart: 8, of which 6 were waited for; matrix products, arithmetic and copies ran while one was open for 35% of the time, Pallas kernels for 0%

profile of v1, /device:TPU:0, one launch (start us, length us, event | category | flops | bytes accessed | tf_op | source)
XLA Modules:
  0.0 421.6 jit_solution(17541238209569439025)
XLA Ops:
  20.7 32.4 %all-to-all-done = bf16[256,4,1536]{0,2,1:T(8,128)(2,1)S(1)} async-done(((bf16[256,4,1536]{0,2,1:T(8,128)(2,1)}), bf16[256,4,1536]{0,2,1:T(8,128)(2,1)S(1)}, u32[]{:S(2)}, u32[]{:S(2)}) %all-to-all-start) | async-done | bytes 3145760 | tf_op jit(solution)/shard_map/all_to_all | solution.py:39
  53.1 4.8 %all-to-all-start.4 = ((bf16[256,4,1536]{0,2,1:T(8,128)(2,1)}), bf16[256,4,1536]{0,2,1:T(8,128)(2,1)}, u32[]{:S(2)}, u32[]{:S(2)}) async-start(bf16[256,4,1536]{0,2,1:T(8,128)(2,1)} %bitcast.125), calls=%async_computation.4 | async-start | bytes 6291456 | tf_op jit(solution)/shard_map/all_to_all | solution.py:36
  59.6 35.2 %all-to-all-done.4 = bf16[256,4,1536]{0,2,1:T(8,128)(2,1)} async-done(((bf16[256,4,1536]{0,2,1:T(8,128)(2,1)}), bf16[256,4,1536]{0,2,1:T(8,128)(2,1)}, u32[]{:S(2)}, u32[]{:S(2)}) %all-to-all-start.4) | async-done | bytes 3145760 | tf_op jit(solution)/shard_map/all_to_all | solution.py:36
  99.4 7.1 %fusion.16 = f32[12,1,128,128]{3,1,2,0:T(1,128)} fusion(f32[4,12,128,128]{3,2,1,0:T(8,128)S(1)} %fusion.13, f32[12,4,1,1]{1,0,2,3:T(8,128)S(1)} %get-tuple-element.257), kind=kOutput, calls=%fused_computation.30 | convolution fusion | flops 9437184 | bytes 3932352 | tf_op jit(solution)/shard_map/hm,mhde->hde/dot_general | solution.py:93
  111.1 4.7 %all-to-all-start.1 = ((bf16[256,4,1536]{0,2,1:T(8,128)(2,1)}), bf16[256,4,1536]{0,2,1:T(8,128)(2,1)}, u32[]{:S(2)}, u32[]{:S(2)}) async-start(bf16[256,4,1536]{0,2,1:T(8,128)(2,1)} %bitcast.127), calls=%async_computation.1 | async-start | bytes 6291456 | tf_op jit(solution)/shard_map/all_to_all | solution.py:38
  115.8 4.7 %copy.73 = bf16[256,6144]{0,1:T(8,128)(2,1)} copy(bf16[256,6144]{1,0:T(8,128)(2,1)} %param.10) | data formatting | bytes 6291456 | tf_op jit(solution)/shard_map/all_to_all | solution.py:37
  120.5 32.2 %all-to-all-done.1 = bf16[256,4,1536]{0,2,1:T(8,128)(2,1)} async-done(((bf16[256,4,1536]{0,2,1:T(8,128)(2,1)}), bf16[256,4,1536]{0,2,1:T(8,128)(2,1)}, u32[]{:S(2)}, u32[]{:S(2)}) %all-to-all-start.1) | async-done | bytes 3145760 | tf_op jit(solution)/shard_map/all_to_all | solution.py:38
  152.7 40.6 %all_to_all.101 = bf16[256,4,1536]{0,2,1:T(8,128)(2,1)S(1)} all-to-all(bf16[256,4,1536]{0,2,1:T(8,128)(2,1)} %bitcast.129), channel_id=1, replica_groups=mesh['ctx'=8,'head'=4] {'head'}, dimensions={1} | all-to-all | bytes 6291456 | tf_op jit(solution)/shard_map/all_to_all | solution.py:37
  199.0 7.1 %fusion.20 = f32[12,1,128,128]{3,1,2,0:T(1,128)} fusion(f32[4,12,128,128]{3,2,1,0:T(8,128)S(1)} %fusion.12, f32[12,4,1,1]{1,0,2,3:T(8,128)S(1)} %get-tuple-element.259), kind=kOutput, calls=%fused_computation.34 | convolution fusion | flops 9437184 | bytes 3932352 | tf_op jit(solution)/shard_map/hm,mhde->hde/dot_general | solution.py:92
  206.1 23.3 %all-reduce = f32[96]{0:T(128)S(1)} all-reduce(f32[96]{0:T(128)S(1)} %get-tuple-element.249), channel_id=2, replica_groups=mesh['ctx'=8,'head'=4] {'ctx'}, use_global_device_ids=true, to_apply=%add | all-reduce | flops 96 | bytes 768
  230.2 4.9 %multiply_convert_fusion.1 = bf16[4,12,256,256]{3,2,1,0:T(8,128)(2,1)S(1)} fusion(f32[12,256,256]{2,1,0:T(8,128)S(1)} %exponential_select_fusion, bf16[4,256,12,128]{1,3,2,0:T(8,128)(2,1)S(1)} %bitcast.117, bf16[4,256,12,128]{1,3,2,0:T(8,128)(2,1)} %bitcast.5), kind=kOutput, calls=%fused_computation.7 | convolution fusion | flops 811597824 | bytes 15728640 | tf_op jit(solution)/shard_map/nihd,njhd->nhij/dot_general | solution.py:57
  237.7 5.5 %fusion.63 = f32[4,12,256,128]{2,3,1,0:T(8,128)} fusion(bf16[4,256,12,128]{1,3,2,0:T(8,128)(2,1)} %bitcast.30, bf16[4,12,256,256]{3,2,1,0:T(8,128)(2,1)S(1)} %multiply_convert_fusion.1), kind=kOutput, calls=%fused_computation.86 | convolution fusion | flops 805306368 | bytes 15728640 | tf_op jit(solution)/shard_map/nhij,nihd->njhd/dot_general | solution.py:116
  243.2 6.2 %rev.7 = f32[8,12,128,128]{3,2,1,0:T(8,128)} reverse(f32[8,12,128,128]{3,2,1,0:T(8,128)} %bitcast.131), dimensions={0} | reverse | bytes 12582912 | tf_op jit(solution)/shard_map/rev | solution.py:15
  249.5 16.9 %while.29 = (s32[]{:T(128)}, f32[12,128,128]{2,1,0:T(8,128)}, s32[]{:T(128)}, f32[8,12]{1,0:T(8,128)S(1)}, f32[8,12,128,128]{3,2,1,0:T(8,128)}, /*index=5*/s32[]{:T(128)}, s32[]{:T(128)}) while((s32[]{:T(128)}, f32[12,128,128]{2,1,0:T(8,128)}, s32[]{:T(128)}, f32[8,12]{1,0:T(8,128)S(1)}, f32[8,12,128,128]{3,2,1,0:T(8,128)}, ...), condition=%wide.region_3.4_spmd.clone, body=%wide.region_2.3_spmd.clone.sunk | while | flops 786436 | bytes 2359545 | solution.py:25
  266.4 10.8 %fusion.32 = bf16[4,12,128,128]{3,0,2,1:T(4,128)(2,1)} fusion(f32[12,4]{1,0:T(8,128)S(1)} %get-tuple-element.260, f32[12,128,128]{2,1,0:T(8,128)} %get-tuple-element.192, f32[4,12,128,128]{3,2,1,0:T(8,128)} %copy-done.4, f32[4,4]{1,0:T(4,128)S(1)} %add_maximum_fusion, f32[12]{0:T(128)S(1)} %broadcast_multiply_fusion, pred[4,4]{1,0:T(4,128)(4,1)S(1)} %fusion.57), kind=kOutput, calls=%fused_computation.40 | convolution fusion | flops 40108416 | bytes 5505344 | tf_op jit(solution)/shard_map/hnm,mhde->nhde/dot_general | solution.py:101
  281.0 6.9 %fusion.6 = bf16[4,256,12,128]{1,3,2,0:T(8,128)(2,1)} fusion(f32[4,12,256,128]{2,3,1,0:T(8,128)} %fusion.63, f32[256,12]{0,1:T(8,128)S(1)} %get-tuple-element.262, bf16[4,12,128,128]{2,3,1,0:T(8,128)(2,1)} %copy.55, bf16[4,256,12,128]{1,3,2,0:T(8,128)(2,1)} %bitcast.5), kind=kOutput, calls=%fused_computation.14 | convolution fusion | flops 407371776 | bytes 14168064 | tf_op jit(solution)/shard_map/njhe,nhde->njhd/dot_general | solution.py:118
  287.9 4.9 %all-to-all-start.5 = ((bf16[4,256,1536]{1,2,0:T(8,128)(2,1)}), bf16[4,256,1536]{1,2,0:T(8,128)(2,1)}, u32[]{:S(2)}, u32[]{:S(2)}) async-start(bf16[4,256,1536]{1,2,0:T(8,128)(2,1)} %bitcast.130), calls=%async_computation.5 | async-start | bytes 6291456 | tf_op jit(solution)/shard_map/all_to_all | solution.py:146
  292.8 8.5 %fusion.62 = f32[4,12,256,128]{2,3,1,0:T(8,128)} fusion(bf16[4,12,256,256]{3,2,1,0:T(8,128)(2,1)} %copy-done.1, bf16[4,256,12,128]{1,3,2,0:T(8,128)(2,1)} %bitcast.121), kind=kOutput, calls=%fused_computation.85 | convolution fusion | flops 805306368 | bytes 15728640 | tf_op jit(solution)/shard_map/nhij,njhd->nihd/dot_general | solution.py:108
  301.3 9.1 %fusion.2 = f32[4,12,256,128]{2,3,1,0:T(8,128)} fusion(bf16[4,256,12,128]{1,3,2,0:T(8,128)(2,1)S(1)} %bitcast.118, f32[12,256,256]{2,1,0:T(8,128)} %copy-done.2, bf16[4,256,12,128]{1,3,2,0:T(8,128)(2,1)} %bitcast.30, bf16[4,256,12,128]{1,3,2,0:T(8,128)(2,1)} %bitcast.122), kind=kOutput, calls=%fused_computation.8 | convolution fusion | flops 1616904192 | bytes 18874368 | tf_op jit(solution)/shard_map/nhij,nihe->njhe/dot_general | solution.py:121
  310.3 6.9 %fusion.4 = bf16[4,256,12,128]{1,3,2,0:T(8,128)(2,1)} fusion(f32[4,12,256,128]{2,3,1,0:T(8,128)} %fusion.2, f32[256,12]{0,1:T(8,128)S(1)} %get-tuple-element.262, bf16[4,12,128,128]{2,3,1,0:T(8,128)(2,1)} %copy.55, bf16[4,256,12,128]{1,3,2,0:T(8,128)(2,1)} %bitcast.123), kind=kOutput, calls=%fused_computation.11 | convolution fusion | flops 407371776 | bytes 14168064 | tf_op jit(solution)/shard_map/njhd,nhde->njhe/dot_general | solution.py:126
  317.3 12.3 %all-to-all-done.5 = bf16[4,256,1536]{1,2,0:T(8,128)(2,1)} async-done(((bf16[4,256,1536]{1,2,0:T(8,128)(2,1)}), bf16[4,256,1536]{1,2,0:T(8,128)(2,1)}, u32[]{:S(2)}, u32[]{:S(2)}) %all-to-all-start.5) | async-done | bytes 3145760 | tf_op jit(solution)/shard_map/all_to_all | solution.py:146
  334.2 16.9 %while.28 = (s32[]{:T(128)}, f32[12,128,128]{2,1,0:T(8,128)}, s32[]{:T(128)}, f32[8,12]{1,0:T(8,128)S(1)}, f32[8,12,128,128]{3,2,1,0:T(8,128)}, /*index=5*/s32[]{:T(128)}, s32[]{:T(128)}) while((s32[]{:T(128)}, f32[12,128,128]{2,1,0:T(8,128)}, s32[]{:T(128)}, f32[8,12]{1,0:T(8,128)S(1)}, f32[8,12,128,128]{3,2,1,0:T(8,128)}, ...), condition=%wide.region_1.2_spmd.clone, body=%wide.region_0.1_spmd.clone.sunk | while | flops 786436 | bytes 2359545 | solution.py:25
  351.1 10.0 %fusion.29 = bf16[4,12,128,128]{3,0,2,1:T(4,128)(2,1)S(1)} fusion(f32[12,4]{1,0:T(8,128)S(1)} %get-tuple-element.258, f32[12,128,128]{2,1,0:T(8,128)} %get-tuple-element.191, f32[4,12,128,128]{3,2,1,0:T(8,128)} %copy-done.3, f32[4,4]{1,0:T(4,128)S(1)} %add_maximum_fusion.1, f32[12]{0:T(128)S(1)} %broadcast_multiply_fusion, pred[4,4]{1,0:T(4,128)(4,1)S(1)} %fusion.58), kind=kOutput, calls=%fused_computation.39 | convolution fusion | flops 40108416 | bytes 5505344 | tf_op jit(solution)/shard_map/hnm,mhde->nhde/dot_general | solution.py:98
  384.1 27.6 %all-to-all-done.3 = bf16[4,256,1536]{1,2,0:T(8,128)(2,1)S(1)} async-done(((bf16[4,256,1536]{1,2,0:T(8,128)(2,1)}), bf16[4,256,1536]{1,2,0:T(8,128)(2,1)S(1)}, u32[]{:S(2)}, u32[]{:S(2)}) %all-to-all-start.3) | async-done | bytes 3145760 | tf_op jit(solution)/shard_map/all_to_all | solution.py:132
  (84 shorter events, 101.1 us)
Async XLA Ops:
  11.8 41.3 %all-to-all-start = ((bf16[256,4,1536]{0,2,1:T(8,128)(2,1)}), bf16[256,4,1536]{0,2,1:T(8,128)(2,1)S(1)}, u32[]{:S(2)}, u32[]{:S(2)}) async-start(bf16[256,4,1536]{0,2,1:T(8,128)(2,1)} %bitcast.128), calls=%async_computation | async-start | bytes 6291456 | tf_op jit(solution)/shard_map/all_to_all | solution.py:39
  53.1 4.9 %copy-start.6 = (u32[32]{0:T(128)S(1)}, u32[32]{0:T(128)}, u32[]{:S(2)}) copy-start(u32[32]{0:T(128)} %constant.87) | copy-start | bytes 388
  53.1 6.1 %copy-start.5 = (f32[48]{0:T(128)S(1)}, f32[48]{0:T(128)}, u32[]{:S(2)}) copy-start(f32[48]{0:T(128)} %param.13) | copy-start | bytes 580
  53.1 41.8 %all-to-all-start.4 = ((bf16[256,4,1536]{0,2,1:T(8,128)(2,1)}), bf16[256,4,1536]{0,2,1:T(8,128)(2,1)}, u32[]{:S(2)}, u32[]{:S(2)}) async-start(bf16[256,4,1536]{0,2,1:T(8,128)(2,1)} %bitcast.125), calls=%async_computation.4 | async-start | bytes 6291456 | tf_op jit(solution)/shard_map/all_to_all | solution.py:36
  57.9 185.4 %all-gather.8.cloned.1.call-start = ((), (), s32[]{:S(2)}) async-start(), calls=%async_computation.8 | async-start | bytes 7077888 | tf_op jit(solution)/shard_map/all_gather | solution.py:13
  97.7 1.7 copy-start.4
  111.1 41.6 %all-to-all-start.1 = ((bf16[256,4,1536]{0,2,1:T(8,128)(2,1)}), bf16[256,4,1536]{0,2,1:T(8,128)(2,1)}, u32[]{:S(2)}, u32[]{:S(2)}) async-start(bf16[256,4,1536]{0,2,1:T(8,128)(2,1)} %bitcast.127), calls=%async_computation.1 | async-start | bytes 6291456 | tf_op jit(solution)/shard_map/all_to_all | solution.py:38
  115.8 218.4 %all-gather.6.cloned.1.call-start = ((), (), s32[]{:S(2)}) async-start(), calls=%async_computation.7 | async-start | bytes 7077888 | tf_op jit(solution)/shard_map/all_gather | solution.py:13
  193.3 4.1 copy-start
  197.4 1.7 copy-start.3
  230.2 4.9 %copy-start.2 = (f32[12,256,256]{2,1,0:T(8,128)}, f32[12,256,256]{2,1,0:T(8,128)S(1)}, u32[]{:S(2)}) copy-start(f32[12,256,256]{2,1,0:T(8,128)S(1)} %exponential_select_fusion) | copy-start | bytes 9437188
  235.1 2.6 copy-start.1
  287.9 41.6 %all-to-all-start.5 = ((bf16[4,256,1536]{1,2,0:T(8,128)(2,1)}), bf16[4,256,1536]{1,2,0:T(8,128)(2,1)}, u32[]{:S(2)}, u32[]{:S(2)}) async-start(bf16[4,256,1536]{1,2,0:T(8,128)(2,1)} %bitcast.130), calls=%async_computation.5 | async-start | bytes 6291456 | tf_op jit(solution)/shard_map/all_to_all | solution.py:146
  329.5 41.6 %all-to-all-start.6 = ((bf16[4,256,1536]{1,2,0:T(8,128)(2,1)}), bf16[4,256,1536]{1,2,0:T(8,128)(2,1)}, u32[]{:S(2)}, u32[]{:S(2)}) async-start(bf16[4,256,1536]{1,2,0:T(8,128)(2,1)} %bitcast.124), calls=%async_computation.6 | async-start | bytes 6291456 | tf_op jit(solution)/shard_map/all_to_all | solution.py:153
  371.1 40.6 %all-to-all-start.3 = ((bf16[4,256,1536]{1,2,0:T(8,128)(2,1)}), bf16[4,256,1536]{1,2,0:T(8,128)(2,1)S(1)}, u32[]{:S(2)}, u32[]{:S(2)}) async-start(bf16[4,256,1536]{1,2,0:T(8,128)(2,1)} %pad_maximum_fusion), calls=%async_computation.3 | async-start | bytes 6291456 | tf_op jit(solution)/shard_map/all_to_all | solution.py:132
Sparse Core Ops, SparseCore 0:
  106.6 99.7 all-gather.7
  208.6 97.6 all-gather.5
